TPU v7x, 256 devices: a whole 4x4x8 slice. The times are simulated.
256 devices in a mesh: rows: 16 (over z, core), cols: 16 (over y, x).
Axes of the slice: x: 4, y: 4, z: 8, core: 2. Of those that a mesh axis runs over, the one named last changes fastest.
Arguments:
- tensor: float32 [32, 2048, 2048], P(None, 'rows', 'cols'), may hold values from -819200 to 819200
- second_init: float32 [2048, 64], P('cols'), may hold values from -6 to 6
- third_init: float32 [32, 64], replicated, may hold values from -6 to 6
Outputs:
- first: float32 [2048, 64], P('rows')
- second: float32 [2048, 64], P('cols')
- third: float32 [32, 64], replicated
All inputs are finite; a program needn't handle non-finite values.
Results may differ from a plain program's by a relative error of at most 0.0003.
Values sent between devices are 32-bit elements; how exact they have to be, the bound alone decides.
No kernel may reach another device: no remote copies, remote signals or barrier semaphores. Data moves between devices by JAX's collectives and lax.ppermute only.
A program may use at most 64 MiB of HBM per device.

v0:
```python
import jax
import jax.numpy as jnp
from jax import lax
from jax.sharding import PartitionSpec as P

ITERS = 5
EPSILON = 1e-05
HIGHEST = lax.Precision.HIGHEST


def solve_right(rhs_rows, system):
    cholesky_low = jnp.linalg.cholesky(system)
    halfway = lax.linalg.triangular_solve(
        cholesky_low, rhs_rows, left_side=False, lower=True, transpose_a=True
    )
    return lax.linalg.triangular_solve(cholesky_low, halfway, left_side=False, lower=True)


def gram_local(factor):
    return jnp.dot(factor.T, factor, precision=HIGHEST, preferred_element_type=jnp.float32)


def settle(raw_share, total_rows):
    squares = lax.psum(jnp.sum(raw_share * raw_share, axis=0), ("rows", "cols"))
    col_scale = jnp.sqrt(squares / total_rows + EPSILON)
    normed = raw_share / col_scale
    gram_whole = lax.psum(gram_local(normed), ("rows", "cols"))
    return (col_scale, gram_whole)


def per_device(tensor, second_init, third_init):
    rows_here = tensor.shape[1]
    cols_here = tensor.shape[2]
    total_first = rows_here * lax.axis_size("rows")
    total_second = cols_here * lax.axis_size("cols")
    share_first = rows_here // lax.axis_size("cols")
    share_second = cols_here // lax.axis_size("rows")
    start_first = lax.axis_index("cols") * share_first
    start_second = lax.axis_index("rows") * share_second
    col_scale, gram_second = settle(
        lax.dynamic_slice_in_dim(second_init, start_second, share_second, 0), total_second
    )
    second = second_init / col_scale
    third = third_init
    gram_third = gram_local(third)
    first = None
    for sweep_index in range(ITERS):
        contract_first = lax.dot_general(
            second,
            tensor,
            (((0,), (2,)), ((), ())),
            precision=HIGHEST,
            preferred_element_type=jnp.float32,
        )
        system_first = gram_third * gram_second
        gram_first = None
        partial_first = jnp.einsum("rki,kr->ir", contract_first, third, precision=HIGHEST)
        mttkrp_first = lax.psum(partial_first, "cols")
        raw_block = solve_right(mttkrp_first, system_first)
        col_scale, gram_first = settle(
            lax.dynamic_slice_in_dim(raw_block, start_first, share_first, 0), total_first
        )
        carried_first = raw_block / col_scale
        contract_second = lax.dot_general(
            carried_first,
            tensor,
            (((0,), (1,)), ((), ())),
            precision=HIGHEST,
            preferred_element_type=jnp.float32,
        )
        partial_second = jnp.einsum("rkj,kr->jr", contract_second, third, precision=HIGHEST)
        outgoing = partial_second
        summed_second = lax.psum(outgoing, "rows")
        first = carried_first
        system_second = gram_third * gram_first
        raw_block = solve_right(summed_second, system_second)
        raw_part = lax.dynamic_slice_in_dim(raw_block, start_second, share_second, 0)
        col_scale, gram_second = settle(raw_part, total_second)
        carried_second = raw_block / col_scale
        partial_third = jnp.einsum("rkj,jr->kr", contract_second, carried_second, precision=HIGHEST)
        outgoing = partial_third
        summed_third = lax.psum(outgoing, ("rows", "cols"))
        second = carried_second
        third = solve_right(summed_third, gram_first * gram_second)
        gram_third = gram_local(third)
    return (first, second, third)


def solution(mesh):
    return jax.shard_map(
        per_device,
        mesh=mesh,
        in_specs=(P(None, "rows", "cols"), P("cols", None), P()),
        out_specs=(P("rows", None), P("cols", None), P()),
        check_vma=False,
    )
```

profile of v0, /device:TPU:1, one launch (start us, length us, event | category | flops | bytes accessed | tf_op | source)
XLA Modules:
  0.0 2455.2 jit_solution(10629154190226435686)
XLA Ops:
  1.7 81.4 %psum.259 = f32[64]{0:T(128)S(1)} all-reduce(f32[64]{0:T(128)S(1)} %multiply_reduce_fusion.10), channel_id=1, replica_groups=mesh['rows'=16,'cols'=16] {'rows','cols'}, use_global_device_ids=true, to_apply=%region_1.0 | all-reduce | flops 64 | bytes 512 | tf_op jit(solution)/shard_map/psum | solution.py:24
  85.1 72.8 %psum.260 = f32[64,64]{0,1:T(8,128)S(1)} all-reduce(f32[64,64]{0,1:T(8,128)S(1)} %fusion.163), channel_id=1, replica_groups=mesh['rows'=16,'cols'=16] {'rows','cols'}, use_global_device_ids=true, to_apply=%region_2.0 | all-reduce | flops 4096 | bytes 32768 | tf_op jit(solution)/shard_map/psum | solution.py:27
  159.0 5.8 cholesky.239
  166.2 4.9 custom-call.41
  171.1 3.2 fusion.109
  175.8 56.8 %psum.261 = f32[128,64]{0,1:T(8,128)S(1)} all-reduce(f32[128,64]{0,1:T(8,128)S(1)} %bitcast.449), channel_id=1, replica_groups=mesh['rows'=16,'cols'=16] {'cols'}, use_global_device_ids=true, to_apply=%region_5.0 | all-reduce | flops 8192 | bytes 65536 | tf_op jit(solution)/shard_map/psum | solution.py:58
  233.2 86.1 %psum.262 = f32[64]{0:T(128)S(1)} all-reduce(f32[64]{0:T(128)S(1)} %multiply_reduce_fusion.9), channel_id=1, replica_groups=mesh['rows'=16,'cols'=16] {'rows','cols'}, use_global_device_ids=true, to_apply=%region_7.11 | all-reduce | flops 64 | bytes 512 | tf_op jit(solution)/shard_map/psum | solution.py:24
  319.6 73.9 %psum.263 = f32[64,64]{0,1:T(8,128)S(1)} all-reduce(f32[64,64]{0,1:T(8,128)S(1)} %fusion.160), channel_id=1, replica_groups=mesh['rows'=16,'cols'=16] {'rows','cols'}, use_global_device_ids=true, to_apply=%region_8.12 | all-reduce | flops 4096 | bytes 32768 | tf_op jit(solution)/shard_map/psum | solution.py:27
  393.6 5.8 cholesky.250
  400.8 4.9 custom-call.43
  408.5 44.1 %psum.264 = f32[128,64]{0,1:T(8,128)S(1)} all-reduce(f32[128,64]{0,1:T(8,128)S(1)} %bitcast.450), channel_id=1, replica_groups=mesh['rows'=16,'cols'=16] {'rows'}, use_global_device_ids=true, to_apply=%region_9.13 | all-reduce | flops 8192 | bytes 65536 | tf_op jit(solution)/shard_map/psum | solution.py:73
  453.3 76.4 %psum.265 = f32[64]{0:T(128)S(1)} all-reduce(f32[64]{0:T(128)S(1)} %multiply_reduce_fusion.8), channel_id=1, replica_groups=mesh['rows'=16,'cols'=16] {'rows','cols'}, use_global_device_ids=true, to_apply=%region_11.15 | all-reduce | flops 64 | bytes 512 | tf_op jit(solution)/shard_map/psum | solution.py:24
  532.2 74.2 %all-reduce.4 = (f32[32,64]{0,1:T(8,128)S(1)}, f32[64,64]{0,1:T(8,128)S(1)}) all-reduce(f32[32,64]{0,1:T(8,128)S(1)} %bitcast.444, f32[64,64]{0,1:T(8,128)S(1)} %fusion.157), channel_id=1, replica_groups=mesh['rows'=16,'cols'=16] {'rows','cols'}, use_global_device_ids=true, to_apply=%region_13.17 | all-reduce | flops 6144 | bytes 49152 | tf_op jit(solution)/shard_map/psum | solution.py:82
  606.5 5.8 cholesky.261
  613.7 4.9 custom-call.45
  619.5 5.8 cholesky.272
  626.7 4.9 custom-call.47
  635.5 56.8 %psum.268 = f32[128,64]{0,1:T(8,128)S(1)} all-reduce(f32[128,64]{0,1:T(8,128)S(1)} %bitcast.451), channel_id=1, replica_groups=mesh['rows'=16,'cols'=16] {'cols'}, use_global_device_ids=true, to_apply=%region_14.20 | all-reduce | flops 8192 | bytes 65536 | tf_op jit(solution)/shard_map/psum | solution.py:58
  692.9 85.3 %psum.269 = f32[64]{0:T(128)S(1)} all-reduce(f32[64]{0:T(128)S(1)} %multiply_reduce_fusion.7), channel_id=1, replica_groups=mesh['rows'=16,'cols'=16] {'rows','cols'}, use_global_device_ids=true, to_apply=%region_16.22 | all-reduce | flops 64 | bytes 512 | tf_op jit(solution)/shard_map/psum | solution.py:24
  778.5 74.9 %psum.270 = f32[64,64]{0,1:T(8,128)S(1)} all-reduce(f32[64,64]{0,1:T(8,128)S(1)} %fusion.155), channel_id=1, replica_groups=mesh['rows'=16,'cols'=16] {'rows','cols'}, use_global_device_ids=true, to_apply=%region_17.23 | all-reduce | flops 4096 | bytes 32768 | tf_op jit(solution)/shard_map/psum | solution.py:27
  853.5 5.8 cholesky.283
  860.7 4.9 custom-call.49
  868.3 43.4 %psum.271 = f32[128,64]{0,1:T(8,128)S(1)} all-reduce(f32[128,64]{0,1:T(8,128)S(1)} %bitcast.452), channel_id=1, replica_groups=mesh['rows'=16,'cols'=16] {'rows'}, use_global_device_ids=true, to_apply=%region_18.24 | all-reduce | flops 8192 | bytes 65536 | tf_op jit(solution)/shard_map/psum | solution.py:73
  912.2 76.4 %psum.272 = f32[64]{0:T(128)S(1)} all-reduce(f32[64]{0:T(128)S(1)} %multiply_reduce_fusion.6), channel_id=1, replica_groups=mesh['rows'=16,'cols'=16] {'rows','cols'}, use_global_device_ids=true, to_apply=%region_20.26 | all-reduce | flops 64 | bytes 512 | tf_op jit(solution)/shard_map/psum | solution.py:24
  991.2 74.1 %all-reduce.3 = (f32[32,64]{0,1:T(8,128)S(1)}, f32[64,64]{0,1:T(8,128)S(1)}) all-reduce(f32[32,64]{0,1:T(8,128)S(1)} %bitcast.445, f32[64,64]{0,1:T(8,128)S(1)} %fusion.152), channel_id=1, replica_groups=mesh['rows'=16,'cols'=16] {'rows','cols'}, use_global_device_ids=true, to_apply=%region_22.28 | all-reduce | flops 6144 | bytes 49152 | tf_op jit(solution)/shard_map/psum | solution.py:82
  1065.4 5.8 cholesky.294
  1072.6 4.9 custom-call.51
  1078.4 5.8 cholesky.305
  1085.6 4.9 custom-call.53
  1094.4 56.8 %psum.275 = f32[128,64]{0,1:T(8,128)S(1)} all-reduce(f32[128,64]{0,1:T(8,128)S(1)} %bitcast.453), channel_id=1, replica_groups=mesh['rows'=16,'cols'=16] {'cols'}, use_global_device_ids=true, to_apply=%region_23.29 | all-reduce | flops 8192 | bytes 65536 | tf_op jit(solution)/shard_map/psum | solution.py:58
  1151.8 85.3 %psum.276 = f32[64]{0:T(128)S(1)} all-reduce(f32[64]{0:T(128)S(1)} %multiply_reduce_fusion.5), channel_id=1, replica_groups=mesh['rows'=16,'cols'=16] {'rows','cols'}, use_global_device_ids=true, to_apply=%region_25.31 | all-reduce | flops 64 | bytes 512 | tf_op jit(solution)/shard_map/psum | solution.py:24
  1237.3 74.7 %psum.277 = f32[64,64]{0,1:T(8,128)S(1)} all-reduce(f32[64,64]{0,1:T(8,128)S(1)} %fusion.150), channel_id=1, replica_groups=mesh['rows'=16,'cols'=16] {'rows','cols'}, use_global_device_ids=true, to_apply=%region_26.32 | all-reduce | flops 4096 | bytes 32768 | tf_op jit(solution)/shard_map/psum | solution.py:27
  1312.1 5.8 cholesky.316
  1319.3 4.9 custom-call.55
  1326.9 43.3 %psum.278 = f32[128,64]{0,1:T(8,128)S(1)} all-reduce(f32[128,64]{0,1:T(8,128)S(1)} %bitcast.454), channel_id=1, replica_groups=mesh['rows'=16,'cols'=16] {'rows'}, use_global_device_ids=true, to_apply=%region_27.33 | all-reduce | flops 8192 | bytes 65536 | tf_op jit(solution)/shard_map/psum | solution.py:73
  1370.9 76.4 %psum.279 = f32[64]{0:T(128)S(1)} all-reduce(f32[64]{0:T(128)S(1)} %multiply_reduce_fusion.4), channel_id=1, replica_groups=mesh['rows'=16,'cols'=16] {'rows','cols'}, use_global_device_ids=true, to_apply=%region_29.35 | all-reduce | flops 64 | bytes 512 | tf_op jit(solution)/shard_map/psum | solution.py:24
  1449.8 74.3 %all-reduce.2 = (f32[32,64]{0,1:T(8,128)S(1)}, f32[64,64]{0,1:T(8,128)S(1)}) all-reduce(f32[32,64]{0,1:T(8,128)S(1)} %bitcast.446, f32[64,64]{0,1:T(8,128)S(1)} %fusion.147), channel_id=1, replica_groups=mesh['rows'=16,'cols'=16] {'rows','cols'}, use_global_device_ids=true, to_apply=%region_31.37 | all-reduce | flops 6144 | bytes 49152 | tf_op jit(solution)/shard_map/psum | solution.py:82
  1524.3 5.8 cholesky.327
  1531.5 4.9 custom-call.57
  1537.3 5.8 cholesky.338
  1544.5 4.9 custom-call.59
  1549.4 2.4 fusion.70
  1553.2 56.8 %psum.282 = f32[128,64]{0,1:T(8,128)S(1)} all-reduce(f32[128,64]{0,1:T(8,128)S(1)} %bitcast.455), channel_id=1, replica_groups=mesh['rows'=16,'cols'=16] {'cols'}, use_global_device_ids=true, to_apply=%region_32.38 | all-reduce | flops 8192 | bytes 65536 | tf_op jit(solution)/shard_map/psum | solution.py:58
  1610.6 85.3 %psum.283 = f32[64]{0:T(128)S(1)} all-reduce(f32[64]{0:T(128)S(1)} %multiply_reduce_fusion.3), channel_id=1, replica_groups=mesh['rows'=16,'cols'=16] {'rows','cols'}, use_global_device_ids=true, to_apply=%region_34.40 | all-reduce | flops 64 | bytes 512 | tf_op jit(solution)/shard_map/psum | solution.py:24
  1696.2 74.6 %psum.284 = f32[64,64]{0,1:T(8,128)S(1)} all-reduce(f32[64,64]{0,1:T(8,128)S(1)} %fusion.145), channel_id=1, replica_groups=mesh['rows'=16,'cols'=16] {'rows','cols'}, use_global_device_ids=true, to_apply=%region_35.41 | all-reduce | flops 4096 | bytes 32768 | tf_op jit(solution)/shard_map/psum | solution.py:27
  1770.9 5.8 cholesky.349
  1778.1 4.9 custom-call.61
  1785.8 43.4 %psum.285 = f32[128,64]{0,1:T(8,128)S(1)} all-reduce(f32[128,64]{0,1:T(8,128)S(1)} %bitcast.456), channel_id=1, replica_groups=mesh['rows'=16,'cols'=16] {'rows'}, use_global_device_ids=true, to_apply=%region_36.42 | all-reduce | flops 8192 | bytes 65536 | tf_op jit(solution)/shard_map/psum | solution.py:73
  1829.7 76.4 %psum.286 = f32[64]{0:T(128)S(1)} all-reduce(f32[64]{0:T(128)S(1)} %multiply_reduce_fusion.2), channel_id=1, replica_groups=mesh['rows'=16,'cols'=16] {'rows','cols'}, use_global_device_ids=true, to_apply=%region_38.44 | all-reduce | flops 64 | bytes 512 | tf_op jit(solution)/shard_map/psum | solution.py:24
  1908.7 74.2 %all-reduce.1 = (f32[32,64]{0,1:T(8,128)S(1)}, f32[64,64]{0,1:T(8,128)S(1)}) all-reduce(f32[32,64]{0,1:T(8,128)S(1)} %bitcast.447, f32[64,64]{0,1:T(8,128)S(1)} %fusion.142), channel_id=1, replica_groups=mesh['rows'=16,'cols'=16] {'rows','cols'}, use_global_device_ids=true, to_apply=%region_40.46 | all-reduce | flops 6144 | bytes 49152 | tf_op jit(solution)/shard_map/psum | solution.py:82
  1982.9 5.8 cholesky.360
  1990.1 4.9 custom-call.63
  1995.9 5.8 cholesky.371
  2003.1 4.9 custom-call.65
  2011.9 56.8 %psum.289 = f32[128,64]{0,1:T(8,128)S(1)} all-reduce(f32[128,64]{0,1:T(8,128)S(1)} %bitcast.457), channel_id=1, replica_groups=mesh['rows'=16,'cols'=16] {'cols'}, use_global_device_ids=true, to_apply=%region_41.47 | all-reduce | flops 8192 | bytes 65536 | tf_op jit(solution)/shard_map/psum | solution.py:58
  2069.3 85.3 %psum.290 = f32[64]{0:T(128)S(1)} all-reduce(f32[64]{0:T(128)S(1)} %multiply_reduce_fusion.1), channel_id=1, replica_groups=mesh['rows'=16,'cols'=16] {'rows','cols'}, use_global_device_ids=true, to_apply=%region_43.49 | all-reduce | flops 64 | bytes 512 | tf_op jit(solution)/shard_map/psum | solution.py:24
  2155.0 74.7 %psum.291 = f32[64,64]{0,1:T(8,128)S(1)} all-reduce(f32[64,64]{0,1:T(8,128)S(1)} %fusion.140), channel_id=1, replica_groups=mesh['rows'=16,'cols'=16] {'rows','cols'}, use_global_device_ids=true, to_apply=%region_44.50 | all-reduce | flops 4096 | bytes 32768 | tf_op jit(solution)/shard_map/psum | solution.py:27
  2229.8 5.8 cholesky.382
  2237.0 4.9 custom-call.67
  2244.6 43.4 %psum.292 = f32[128,64]{0,1:T(8,128)S(1)} all-reduce(f32[128,64]{0,1:T(8,128)S(1)} %bitcast.458), channel_id=1, replica_groups=mesh['rows'=16,'cols'=16] {'rows'}, use_global_device_ids=true, to_apply=%region_45.51 | all-reduce | flops 8192 | bytes 65536 | tf_op jit(solution)/shard_map/psum | solution.py:73
  2288.5 76.4 %psum.293 = f32[64]{0:T(128)S(1)} all-reduce(f32[64]{0:T(128)S(1)} %multiply_reduce_fusion), channel_id=1, replica_groups=mesh['rows'=16,'cols'=16] {'rows','cols'}, use_global_device_ids=true, to_apply=%region_47.53 | all-reduce | flops 64 | bytes 512 | tf_op jit(solution)/shard_map/psum | solution.py:24
  2367.5 73.9 %all-reduce = (f32[32,64]{0,1:T(8,128)S(1)}, f32[64,64]{0,1:T(8,128)S(1)}) all-reduce(f32[32,64]{0,1:T(8,128)S(1)} %bitcast.448, f32[64,64]{0,1:T(8,128)S(1)} %fusion.138), channel_id=1, replica_groups=mesh['rows'=16,'cols'=16] {'rows','cols'}, use_global_device_ids=true, to_apply=%region_49.55 | all-reduce | flops 6144 | bytes 49152 | tf_op jit(solution)/shard_map/psum | solution.py:82
  2441.5 5.8 cholesky.393
  2448.7 4.9 custom-call.69
  (193 shorter events, 77.7 us)
Async XLA Ops:
  0.6 170.5 %copy-start = (f32[32,128,128]{2,1,0:T(8,128)S(1)}, f32[32,128,128]{2,1,0:T(8,128)}, u32[]{:S(2)}) copy-start(f32[32,128,128]{2,1,0:T(8,128)} %param.12) | copy-start | bytes 6291460
  2155.0 89.7 %copy-start.1 = (f32[128,64]{0,1:T(8,128)}, f32[128,64]{0,1:T(8,128)S(1)}, u32[]{:S(2)}) copy-start(f32[128,64]{0,1:T(8,128)S(1)} %broadcast_divide_fusion.1) | copy-start | bytes 98308
  2365.3 89.4 %copy-start.2 = (f32[128,64]{0,1:T(8,128)}, f32[128,64]{0,1:T(8,128)S(1)}, u32[]{:S(2)}) copy-start(f32[128,64]{0,1:T(8,128)S(1)} %broadcast_divide_fusion) | copy-start | bytes 98308
where the time goes:
time: 2470 us; the launch traced here: 2460 us
  blocking collectives  2210 us (89%)
  other arithmetic  185 us (7%)
  matrix products  57.5 us (2%)
    psum x11, blocking collectives, settle(): squares = lax.psum(jnp.sum(raw_share * raw_share, axis=0), ('rows', 'cols'))  891 us
    psum x6, blocking collectives, settle(): gram_whole = lax.psum(gram_local(normed), ('rows', 'cols'))  446 us
    psum x5, blocking collectives, per_device(): summed_third = lax.psum(outgoing, ('rows', 'cols'))  371 us
    psum x5, blocking collectives, per_device(): mttkrp_first = lax.psum(partial_first, 'cols')  284 us
    psum x5, blocking collectives, per_device(): summed_second = lax.psum(outgoing, 'rows')  218 us
    another operation x45, other arithmetic, solve_right(): cholesky_low = jnp.linalg.cholesky(system)  97.8 us
    another operation x30, other arithmetic, solve_right(): lax.linalg.triangular_solve(cholesky_low, halfway, left_side=False, lower...  83.2 us

commit v1 on v0

--- a/solution.py
+++ b/solution.py
@@ -79,7 +79,7 @@
         carried_second = raw_block / col_scale
         partial_third = jnp.einsum("rkj,jr->kr", contract_second, carried_second, precision=HIGHEST)
         outgoing = partial_third
-        summed_third = lax.psum(outgoing, ("rows", "cols"))
+        summed_third = lax.psum(lax.psum(outgoing, "rows"), "cols")
         second = carried_second
         third = solve_right(summed_third, gram_first * gram_second)
         gram_third = gram_local(third)

time: 2470 us -> 3040 us (1.23)
  blocking collectives: 2210 us -> 2790 us
    psum x6 -> x11, blocking collectives: 446 us -> 829 us  [settle(): gram_whole = lax.psum(gram_local(normed), ('rows', 'cols'))]
    psum x5 -> x10, blocking collectives: 371 us -> 506 us  [per_device(): summed_third = lax.psum(lax.psum(outgoing, 'rows'), 'cols')]
    psum x11, blocking collectives: 891 us -> 955 us  [settle(): squares = lax.psum(jnp.sum(raw_share * raw_share, axis=0), ('rows', 'cols'))]
where the time goes in v1:
time: 3040 us; the launch traced here: 3030 us
  blocking collectives  2790 us (92%)
  other arithmetic  185 us (6%)
  matrix products  57.5 us (2%)
    psum x11, blocking collectives, settle(): squares = lax.psum(jnp.sum(raw_share * raw_share, axis=0), ('rows', 'cols'))  955 us
    psum x11, blocking collectives, settle(): gram_whole = lax.psum(gram_local(normed), ('rows', 'cols'))  829 us
    psum x10, blocking collectives, per_device(): summed_third = lax.psum(lax.psum(outgoing, 'rows'), 'cols')  506 us
    psum x5, blocking collectives, per_device(): mttkrp_first = lax.psum(partial_first, 'cols')  280 us
    psum x5, blocking collectives, per_device(): summed_second = lax.psum(outgoing, 'rows')  217 us
    another operation x45, other arithmetic, solve_right(): cholesky_low = jnp.linalg.cholesky(system)  97.8 us
    another operation x30, other arithmetic, solve_right(): lax.linalg.triangular_solve(cholesky_low, halfway, left_side=False, lower...  83.2 us

profile of v1, /device:TPU:1, one launch (start us, length us, event | category | flops | bytes accessed | tf_op | source)
XLA Modules:
  0.0 3033.3 jit_solution(9574835992057540743)
XLA Ops:
  1.7 81.4 %psum.294 = f32[64]{0:T(128)S(1)} all-reduce(f32[64]{0:T(128)S(1)} %multiply_reduce_fusion.10), channel_id=1, replica_groups=mesh['rows'=16,'cols'=16] {'rows','cols'}, use_global_device_ids=true, to_apply=%region_1.0 | all-reduce | flops 64 | bytes 512 | tf_op jit(solution)/shard_map/psum | solution.py:24
  85.1 72.8 %psum.295 = f32[64,64]{0,1:T(8,128)S(1)} all-reduce(f32[64,64]{0,1:T(8,128)S(1)} %fusion.163), channel_id=1, replica_groups=mesh['rows'=16,'cols'=16] {'rows','cols'}, use_global_device_ids=true, to_apply=%region_2.0 | all-reduce | flops 4096 | bytes 32768 | tf_op jit(solution)/shard_map/psum | solution.py:27
  159.0 5.8 cholesky.239
  166.2 4.9 custom-call.41
  175.9 56.8 %psum.296 = f32[128,64]{0,1:T(8,128)S(1)} all-reduce(f32[128,64]{0,1:T(8,128)S(1)} %bitcast.444), channel_id=1, replica_groups=mesh['rows'=16,'cols'=16] {'cols'}, use_global_device_ids=true, to_apply=%region_5.0 | all-reduce | flops 8192 | bytes 65536 | tf_op jit(solution)/shard_map/psum | solution.py:58
  233.2 86.1 %psum.297 = f32[64]{0:T(128)S(1)} all-reduce(f32[64]{0:T(128)S(1)} %multiply_reduce_fusion.9), channel_id=1, replica_groups=mesh['rows'=16,'cols'=16] {'rows','cols'}, use_global_device_ids=true, to_apply=%region_7.11 | all-reduce | flops 64 | bytes 512 | tf_op jit(solution)/shard_map/psum | solution.py:24
  319.6 74.2 %psum.298 = f32[64,64]{0,1:T(8,128)S(1)} all-reduce(f32[64,64]{0,1:T(8,128)S(1)} %fusion.160), channel_id=1, replica_groups=mesh['rows'=16,'cols'=16] {'rows','cols'}, use_global_device_ids=true, to_apply=%region_8.12 | all-reduce | flops 4096 | bytes 32768 | tf_op jit(solution)/shard_map/psum | solution.py:27
  393.9 5.8 cholesky.250
  401.1 4.9 custom-call.43
  408.8 44.1 %psum.299 = f32[128,64]{0,1:T(8,128)S(1)} all-reduce(f32[128,64]{0,1:T(8,128)S(1)} %bitcast.445), channel_id=1, replica_groups=mesh['rows'=16,'cols'=16] {'rows'}, use_global_device_ids=true, to_apply=%region_9.13 | all-reduce | flops 8192 | bytes 65536 | tf_op jit(solution)/shard_map/psum | solution.py:73
  453.5 76.4 %psum.300 = f32[64]{0:T(128)S(1)} all-reduce(f32[64]{0:T(128)S(1)} %multiply_reduce_fusion.8), channel_id=1, replica_groups=mesh['rows'=16,'cols'=16] {'rows','cols'}, use_global_device_ids=true, to_apply=%region_11.15 | all-reduce | flops 64 | bytes 512 | tf_op jit(solution)/shard_map/psum | solution.py:24
  530.3 73.7 %psum.301 = f32[64,64]{0,1:T(8,128)S(1)} all-reduce(f32[64,64]{0,1:T(8,128)S(1)} %fusion.157), channel_id=1, replica_groups=mesh['rows'=16,'cols'=16] {'rows','cols'}, use_global_device_ids=true, to_apply=%region_12.16 | all-reduce | flops 4096 | bytes 32768 | tf_op jit(solution)/shard_map/psum | solution.py:27
  606.2 43.4 %psum.302 = f32[32,64]{0,1:T(8,128)S(1)} all-reduce(f32[32,64]{0,1:T(8,128)S(1)} %bitcast.446), channel_id=1, replica_groups=mesh['rows'=16,'cols'=16] {'rows'}, use_global_device_ids=true, to_apply=%region_13.17 | all-reduce | flops 2048 | bytes 16384 | tf_op jit(solution)/shard_map/psum | solution.py:82
  649.6 57.7 %psum.303 = f32[32,64]{0,1:T(8,128)S(1)} all-reduce(f32[32,64]{0,1:T(8,128)S(1)} %psum.302), channel_id=1, replica_groups=mesh['rows'=16,'cols'=16] {'cols'}, use_global_device_ids=true, to_apply=%region_14.18 | all-reduce | flops 2048 | bytes 16384 | tf_op jit(solution)/shard_map/psum | solution.py:82
  707.3 5.8 cholesky.261
  714.5 4.9 custom-call.45
  720.3 5.8 cholesky.272
  727.5 4.9 custom-call.47
  736.3 55.8 %psum.304 = f32[128,64]{0,1:T(8,128)S(1)} all-reduce(f32[128,64]{0,1:T(8,128)S(1)} %bitcast.447), channel_id=1, replica_groups=mesh['rows'=16,'cols'=16] {'cols'}, use_global_device_ids=true, to_apply=%region_15.21 | all-reduce | flops 8192 | bytes 65536 | tf_op jit(solution)/shard_map/psum | solution.py:58
  792.7 101.4 %psum.305 = f32[64]{0:T(128)S(1)} all-reduce(f32[64]{0:T(128)S(1)} %multiply_reduce_fusion.7), channel_id=1, replica_groups=mesh['rows'=16,'cols'=16] {'rows','cols'}, use_global_device_ids=true, to_apply=%region_17.23 | all-reduce | flops 64 | bytes 512 | tf_op jit(solution)/shard_map/psum | solution.py:24
  894.4 74.7 %psum.306 = f32[64,64]{0,1:T(8,128)S(1)} all-reduce(f32[64,64]{0,1:T(8,128)S(1)} %fusion.155), channel_id=1, replica_groups=mesh['rows'=16,'cols'=16] {'rows','cols'}, use_global_device_ids=true, to_apply=%region_18.24 | all-reduce | flops 4096 | bytes 32768 | tf_op jit(solution)/shard_map/psum | solution.py:27
  969.2 5.8 cholesky.283
  984.0 43.3 %psum.307 = f32[128,64]{0,1:T(8,128)S(1)} all-reduce(f32[128,64]{0,1:T(8,128)S(1)} %bitcast.448), channel_id=1, replica_groups=mesh['rows'=16,'cols'=16] {'rows'}, use_global_device_ids=true, to_apply=%region_19.25 | all-reduce | flops 8192 | bytes 65536 | tf_op jit(solution)/shard_map/psum | solution.py:73
  1027.9 76.4 %psum.308 = f32[64]{0:T(128)S(1)} all-reduce(f32[64]{0:T(128)S(1)} %multiply_reduce_fusion.6), channel_id=1, replica_groups=mesh['rows'=16,'cols'=16] {'rows','cols'}, use_global_device_ids=true, to_apply=%region_21.27 | all-reduce | flops 64 | bytes 512 | tf_op jit(solution)/shard_map/psum | solution.py:24
  1104.7 73.7 %psum.309 = f32[64,64]{0,1:T(8,128)S(1)} all-reduce(f32[64,64]{0,1:T(8,128)S(1)} %fusion.152), channel_id=1, replica_groups=mesh['rows'=16,'cols'=16] {'rows','cols'}, use_global_device_ids=true, to_apply=%region_22.28 | all-reduce | flops 4096 | bytes 32768 | tf_op jit(solution)/shard_map/psum | solution.py:27
  1180.6 43.4 %psum.310 = f32[32,64]{0,1:T(8,128)S(1)} all-reduce(f32[32,64]{0,1:T(8,128)S(1)} %bitcast.449), channel_id=1, replica_groups=mesh['rows'=16,'cols'=16] {'rows'}, use_global_device_ids=true, to_apply=%region_23.29 | all-reduce | flops 2048 | bytes 16384 | tf_op jit(solution)/shard_map/psum | solution.py:82
  1224.0 57.9 %psum.311 = f32[32,64]{0,1:T(8,128)S(1)} all-reduce(f32[32,64]{0,1:T(8,128)S(1)} %psum.310), channel_id=1, replica_groups=mesh['rows'=16,'cols'=16] {'cols'}, use_global_device_ids=true, to_apply=%region_24.30 | all-reduce | flops 2048 | bytes 16384 | tf_op jit(solution)/shard_map/psum | solution.py:82
  1282.0 5.8 cholesky.294
  1295.0 5.8 cholesky.305
  1310.9 55.8 %psum.312 = f32[128,64]{0,1:T(8,128)S(1)} all-reduce(f32[128,64]{0,1:T(8,128)S(1)} %bitcast.450), channel_id=1, replica_groups=mesh['rows'=16,'cols'=16] {'cols'}, use_global_device_ids=true, to_apply=%region_25.31 | all-reduce | flops 8192 | bytes 65536 | tf_op jit(solution)/shard_map/psum | solution.py:58
  1367.3 101.4 %psum.313 = f32[64]{0:T(128)S(1)} all-reduce(f32[64]{0:T(128)S(1)} %multiply_reduce_fusion.5), channel_id=1, replica_groups=mesh['rows'=16,'cols'=16] {'rows','cols'}, use_global_device_ids=true, to_apply=%region_27.33 | all-reduce | flops 64 | bytes 512 | tf_op jit(solution)/shard_map/psum | solution.py:24
  1469.0 74.7 %psum.314 = f32[64,64]{0,1:T(8,128)S(1)} all-reduce(f32[64,64]{0,1:T(8,128)S(1)} %fusion.150), channel_id=1, replica_groups=mesh['rows'=16,'cols'=16] {'rows','cols'}, use_global_device_ids=true, to_apply=%region_28.34 | all-reduce | flops 4096 | bytes 32768 | tf_op jit(solution)/shard_map/psum | solution.py:27
  1543.8 5.8 cholesky.316
  1551.0 4.9 custom-call.55
  1558.6 43.3 %psum.315 = f32[128,64]{0,1:T(8,128)S(1)} all-reduce(f32[128,64]{0,1:T(8,128)S(1)} %bitcast.451), channel_id=1, replica_groups=mesh['rows'=16,'cols'=16] {'rows'}, use_global_device_ids=true, to_apply=%region_29.35 | all-reduce | flops 8192 | bytes 65536 | tf_op jit(solution)/shard_map/psum | solution.py:73
  1602.5 76.4 %psum.316 = f32[64]{0:T(128)S(1)} all-reduce(f32[64]{0:T(128)S(1)} %multiply_reduce_fusion.4), channel_id=1, replica_groups=mesh['rows'=16,'cols'=16] {'rows','cols'}, use_global_device_ids=true, to_apply=%region_31.37 | all-reduce | flops 64 | bytes 512 | tf_op jit(solution)/shard_map/psum | solution.py:24
  1679.3 73.7 %psum.317 = f32[64,64]{0,1:T(8,128)S(1)} all-reduce(f32[64,64]{0,1:T(8,128)S(1)} %fusion.147), channel_id=1, replica_groups=mesh['rows'=16,'cols'=16] {'rows','cols'}, use_global_device_ids=true, to_apply=%region_32.38 | all-reduce | flops 4096 | bytes 32768 | tf_op jit(solution)/shard_map/psum | solution.py:27
  1755.2 43.4 %psum.318 = f32[32,64]{0,1:T(8,128)S(1)} all-reduce(f32[32,64]{0,1:T(8,128)S(1)} %bitcast.452), channel_id=1, replica_groups=mesh['rows'=16,'cols'=16] {'rows'}, use_global_device_ids=true, to_apply=%region_33.39 | all-reduce | flops 2048 | bytes 16384 | tf_op jit(solution)/shard_map/psum | solution.py:82
  1798.6 57.7 %psum.319 = f32[32,64]{0,1:T(8,128)S(1)} all-reduce(f32[32,64]{0,1:T(8,128)S(1)} %psum.318), channel_id=1, replica_groups=mesh['rows'=16,'cols'=16] {'cols'}, use_global_device_ids=true, to_apply=%region_34.40 | all-reduce | flops 2048 | bytes 16384 | tf_op jit(solution)/shard_map/psum | solution.py:82
  1856.4 5.8 cholesky.327
  1869.4 5.8 cholesky.338
  1885.4 55.8 %psum.320 = f32[128,64]{0,1:T(8,128)S(1)} all-reduce(f32[128,64]{0,1:T(8,128)S(1)} %bitcast.453), channel_id=1, replica_groups=mesh['rows'=16,'cols'=16] {'cols'}, use_global_device_ids=true, to_apply=%region_35.41 | all-reduce | flops 8192 | bytes 65536 | tf_op jit(solution)/shard_map/psum | solution.py:58
  1941.7 101.4 %psum.321 = f32[64]{0:T(128)S(1)} all-reduce(f32[64]{0:T(128)S(1)} %multiply_reduce_fusion.3), channel_id=1, replica_groups=mesh['rows'=16,'cols'=16] {'rows','cols'}, use_global_device_ids=true, to_apply=%region_37.43 | all-reduce | flops 64 | bytes 512 | tf_op jit(solution)/shard_map/psum | solution.py:24
  2043.4 74.9 %psum.322 = f32[64,64]{0,1:T(8,128)S(1)} all-reduce(f32[64,64]{0,1:T(8,128)S(1)} %fusion.145), channel_id=1, replica_groups=mesh['rows'=16,'cols'=16] {'rows','cols'}, use_global_device_ids=true, to_apply=%region_38.44 | all-reduce | flops 4096 | bytes 32768 | tf_op jit(solution)/shard_map/psum | solution.py:27
  2118.4 5.8 cholesky.349
  2133.2 43.3 %psum.323 = f32[128,64]{0,1:T(8,128)S(1)} all-reduce(f32[128,64]{0,1:T(8,128)S(1)} %bitcast.454), channel_id=1, replica_groups=mesh['rows'=16,'cols'=16] {'rows'}, use_global_device_ids=true, to_apply=%region_39.45 | all-reduce | flops 8192 | bytes 65536 | tf_op jit(solution)/shard_map/psum | solution.py:73
  2177.1 76.4 %psum.324 = f32[64]{0:T(128)S(1)} all-reduce(f32[64]{0:T(128)S(1)} %multiply_reduce_fusion.2), channel_id=1, replica_groups=mesh['rows'=16,'cols'=16] {'rows','cols'}, use_global_device_ids=true, to_apply=%region_41.47 | all-reduce | flops 64 | bytes 512 | tf_op jit(solution)/shard_map/psum | solution.py:24
  2253.9 73.7 %psum.325 = f32[64,64]{0,1:T(8,128)S(1)} all-reduce(f32[64,64]{0,1:T(8,128)S(1)} %fusion.142), channel_id=1, replica_groups=mesh['rows'=16,'cols'=16] {'rows','cols'}, use_global_device_ids=true, to_apply=%region_42.48 | all-reduce | flops 4096 | bytes 32768 | tf_op jit(solution)/shard_map/psum | solution.py:27
  2329.8 43.4 %psum.326 = f32[32,64]{0,1:T(8,128)S(1)} all-reduce(f32[32,64]{0,1:T(8,128)S(1)} %bitcast.455), channel_id=1, replica_groups=mesh['rows'=16,'cols'=16] {'rows'}, use_global_device_ids=true, to_apply=%region_43.49 | all-reduce | flops 2048 | bytes 16384 | tf_op jit(solution)/shard_map/psum | solution.py:82
  2373.2 57.7 %psum.327 = f32[32,64]{0,1:T(8,128)S(1)} all-reduce(f32[32,64]{0,1:T(8,128)S(1)} %psum.326), channel_id=1, replica_groups=mesh['rows'=16,'cols'=16] {'cols'}, use_global_device_ids=true, to_apply=%region_44.50 | all-reduce | flops 2048 | bytes 16384 | tf_op jit(solution)/shard_map/psum | solution.py:82
  2431.0 5.8 cholesky.360
  2444.0 5.8 cholesky.371
  2451.1 4.9 custom-call.65
  2459.9 55.8 %psum.328 = f32[128,64]{0,1:T(8,128)S(1)} all-reduce(f32[128,64]{0,1:T(8,128)S(1)} %bitcast.456), channel_id=1, replica_groups=mesh['rows'=16,'cols'=16] {'cols'}, use_global_device_ids=true, to_apply=%region_45.51 | all-reduce | flops 8192 | bytes 65536 | tf_op jit(solution)/shard_map/psum | solution.py:58
  2516.3 101.4 %psum.329 = f32[64]{0:T(128)S(1)} all-reduce(f32[64]{0:T(128)S(1)} %multiply_reduce_fusion.1), channel_id=1, replica_groups=mesh['rows'=16,'cols'=16] {'rows','cols'}, use_global_device_ids=true, to_apply=%region_47.53 | all-reduce | flops 64 | bytes 512 | tf_op jit(solution)/shard_map/psum | solution.py:24
  2618.1 74.7 %psum.330 = f32[64,64]{0,1:T(8,128)S(1)} all-reduce(f32[64,64]{0,1:T(8,128)S(1)} %fusion.140), channel_id=1, replica_groups=mesh['rows'=16,'cols'=16] {'rows','cols'}, use_global_device_ids=true, to_apply=%region_48.54 | all-reduce | flops 4096 | bytes 32768 | tf_op jit(solution)/shard_map/psum | solution.py:27
  2692.9 5.8 cholesky.382
  2707.7 43.3 %psum.331 = f32[128,64]{0,1:T(8,128)S(1)} all-reduce(f32[128,64]{0,1:T(8,128)S(1)} %bitcast.457), channel_id=1, replica_groups=mesh['rows'=16,'cols'=16] {'rows'}, use_global_device_ids=true, to_apply=%region_49.55 | all-reduce | flops 8192 | bytes 65536 | tf_op jit(solution)/shard_map/psum | solution.py:73
  2751.7 76.4 %psum.332 = f32[64]{0:T(128)S(1)} all-reduce(f32[64]{0:T(128)S(1)} %multiply_reduce_fusion), channel_id=1, replica_groups=mesh['rows'=16,'cols'=16] {'rows','cols'}, use_global_device_ids=true, to_apply=%region_51.57 | all-reduce | flops 64 | bytes 512 | tf_op jit(solution)/shard_map/psum | solution.py:24
  2830.6 44.2 %psum.334 = f32[32,64]{0,1:T(8,128)S(1)} all-reduce(f32[32,64]{0,1:T(8,128)S(1)} %bitcast.458), channel_id=1, replica_groups=mesh['rows'=16,'cols'=16] {'rows'}, use_global_device_ids=true, to_apply=%region_53.59 | all-reduce | flops 2048 | bytes 16384 | tf_op jit(solution)/shard_map/psum | solution.py:82
  2874.8 57.0 %psum.335 = f32[32,64]{0,1:T(8,128)S(1)} all-reduce(f32[32,64]{0,1:T(8,128)S(1)} %psum.334), channel_id=1, replica_groups=mesh['rows'=16,'cols'=16] {'cols'}, use_global_device_ids=true, to_apply=%region_54.60 | all-reduce | flops 2048 | bytes 16384 | tf_op jit(solution)/shard_map/psum | solution.py:82
  2931.8 88.0 %psum.333 = f32[64,64]{0,1:T(8,128)S(1)} all-reduce(f32[64,64]{0,1:T(8,128)S(1)} %fusion.138), channel_id=1, replica_groups=mesh['rows'=16,'cols'=16] {'rows','cols'}, use_global_device_ids=true, to_apply=%region_52.58 | all-reduce | flops 4096 | bytes 32768 | tf_op jit(solution)/shard_map/psum | solution.py:27
  3019.8 5.8 cholesky.393
  3027.0 4.9 custom-call.69
  (203 shorter events, 122.5 us)
Async XLA Ops:
  0.6 170.5 %copy-start = (f32[32,128,128]{2,1,0:T(8,128)S(1)}, f32[32,128,128]{2,1,0:T(8,128)}, u32[]{:S(2)}) copy-start(f32[32,128,128]{2,1,0:T(8,128)} %param.12) | copy-start | bytes 6291460
  2618.1 89.6 %copy-start.1 = (f32[128,64]{0,1:T(8,128)}, f32[128,64]{0,1:T(8,128)S(1)}, u32[]{:S(2)}) copy-start(f32[128,64]{0,1:T(8,128)S(1)} %broadcast_divide_fusion.1) | copy-start | bytes 98308
  2828.4 204.6 %copy-start.2 = (f32[128,64]{0,1:T(8,128)}, f32[128,64]{0,1:T(8,128)S(1)}, u32[]{:S(2)}) copy-start(f32[128,64]{0,1:T(8,128)S(1)} %broadcast_divide_fusion) | copy-start | bytes 98308
